TPU v7x, 256 devices: a whole 4x4x8 slice. The times are simulated.
256 devices in a mesh: dp: 16 (over y, z_hi, core), tensor: 16 (over z_lo, x).
Axes of the slice: x: 4, y: 4, z: 8 (z_hi: 2, z_lo: 4; z = z_hi * 4 + z_lo), core: 2. Of those that a mesh axis runs over, the one named last changes fastest.
Arguments:
- tokens: bfloat16 [1024, 8192], P('tensor', 'dp'), may hold values from -6 to 6
- gate_weight: bfloat16 [8192, 29568], P('dp', 'tensor'), may hold values from -0.0625 to 0.0625
- up_weight: bfloat16 [8192, 29568], P('dp', 'tensor'), may hold values from -0.0625 to 0.0625
- down_weight: bfloat16 [29568, 8192], P('tensor', 'dp'), may hold values from -0.03125 to 0.03125
- labels: int32 [1024], P('tensor'), may hold values from 0 to 255
Outputs:
- erased: bfloat16 [1024, 8192], P('tensor', 'dp')
All inputs are finite; a program needn't handle non-finite values.
Results may differ from a plain program's by a relative error of at most 0.029.
Values may be sent and summed in bfloat16 or wider, within the bound.
A program may use at most 64 MiB of HBM per device.

v0:
```python
import jax
import jax.numpy as jnp
from jax import lax
from jax.sharding import PartitionSpec as P

NCLS = 256


epsilon = 1e-05
ridge_share = 0.5


def shards(tokens, gate_weight, up_weight, down_weight, labels):
    groups = lax.axis_size("tensor")
    shard_rows = tokens.shape[0]
    row_total = shard_rows * groups
    hidden_cols = gate_weight.shape[1]
    high = lax.Precision.HIGHEST
    gathered = lax.all_gather(tokens, "tensor", axis=0, tiled=True)
    joined = jnp.concatenate([gate_weight, up_weight], axis=1)
    partial_value = jnp.dot(gathered, joined, preferred_element_type=jnp.float32).astype(
        jnp.bfloat16
    )
    summed = lax.psum_scatter(
        lax.optimization_barrier(partial_value).astype(jnp.float32).astype(jnp.bfloat16),
        "dp",
        scatter_dimension=0,
        tiled=True,
    ).astype(jnp.float32)
    hidden = (jax.nn.silu(summed[:, :hidden_cols]) * summed[:, hidden_cols:]).astype(jnp.bfloat16)
    partial_out = jnp.dot(
        lax.all_gather(hidden, "dp", axis=0, tiled=True),
        down_weight,
        preferred_element_type=jnp.float32,
    )
    output = lax.psum_scatter(partial_out, "tensor", scatter_dimension=0, tiled=True)
    classes = jnp.arange(NCLS, dtype=jnp.int32)
    onehot = (labels[:, None] == classes[None, :]).astype(jnp.float32)
    col_total, counts = lax.psum((jnp.sum(output, axis=0), jnp.sum(onehot, axis=0)), "tensor")
    mean_out = col_total / row_total
    shares = counts / row_total
    centred = output - mean_out
    cross_part = jnp.dot(centred.T, onehot - shares, precision=high)
    cross_sum, square_sum = lax.psum((cross_part, jnp.sum(centred * centred, axis=0)), "tensor")
    cross = cross_sum / row_total
    variance = square_sum / row_total
    spread = jnp.sqrt(variance + epsilon)
    whitened = cross / spread[:, None]
    white_rows = centred / spread
    gram_mat, coords = lax.psum(
        (
            jnp.dot(whitened.T, whitened, precision=high),
            jnp.dot(white_rows, whitened, precision=high),
        ),
        "dp",
    )
    ridge_term = ridge_share * jnp.trace(gram_mat) / NCLS
    factor = jnp.linalg.cholesky(gram_mat + ridge_term * jnp.eye(NCLS, dtype=jnp.float32))
    solved = jax.scipy.linalg.cho_solve((factor, True), coords.T)
    correction = jnp.dot(whitened, solved, precision=high).T * spread
    return (output - correction).astype(jnp.bfloat16)


def solution(mesh):
    return jax.shard_map(
        shards,
        mesh=mesh,
        in_specs=(
            P("tensor", "dp"),
            P("dp", "tensor"),
            P("dp", "tensor"),
            P("tensor", "dp"),
            P("tensor"),
        ),
        out_specs=P("tensor", "dp"),
        check_vma=False,
    )
```

profile of v0, /device:TPU:1, one launch (start us, length us, event | category | flops | bytes accessed | tf_op | source)
XLA Modules:
  0.0 900.5 jit_solution(123671681127873409)
XLA Ops:
  6.5 0.7 all-gather.3.cloned.1.call-update
  7.3 76.4 %all-gather.3.cloned.1.call-done = bf16[1024,512]{1,0:T(8,128)(2,1)} async-done(((bf16[64,512]{1,0:T(8,128)(2,1)}), bf16[1024,512]{1,0:T(8,128)(2,1)}) %all-gather.3.cloned.1.call-update) | async-done | bytes 1048592 | tf_op jit(solution)/shard_map/all_gather | solution.py:19
  83.7 9.6 %convert_bitcast_fusion = bf16[1024,3696]{0,1:T(8,128)(2,1)} fusion(bf16[1024,512]{1,0:T(8,128)(2,1)} %all-gather.3.cloned.1.call-done, bf16[512,1848]{0,1:T(8,128)(2,1)} %param.7, bf16[512,1848]{0,1:T(8,128)(2,1)} %param.6), kind=kOutput, calls=%fused_computation.2 | convolution fusion | flops 3886891008 | bytes 12402688 | tf_op jit(solution)/shard_map/dot_general | solution.py:21
  93.3 10.3 %copy.34 = bf16[1024,3696]{1,0:T(8,128)(2,1)} copy(bf16[1024,3696]{0,1:T(8,128)(2,1)} %convert_bitcast_fusion) | data formatting | bytes 15138816
  103.6 138.4 %reduce-scatter.7.cloned.1.call-done = bf16[64,3696]{1,0:T(8,128)(2,1)} async-done(((bf16[1024,3696]{1,0:T(8,128)(2,1)}), bf16[64,3696]{1,0:T(8,128)(2,1)}) %reduce-scatter.7.cloned.1.call-update) | async-done | bytes 473104 | tf_op jit(solution)/shard_map/reduce_scatter | solution.py:24
  242.1 1.1 convert_element_type.23
  243.2 0.9 fusion.5
  244.2 73.9 %all-gather.5.cloned.1.call-done = bf16[1024,1848]{1,0:T(8,128)(2,1)} async-done(((bf16[64,1848]{1,0:T(8,128)(2,1)}), bf16[1024,1848]{1,0:T(8,128)(2,1)}) %all-gather.5.cloned.1.call-update) | async-done | bytes 3784720 | tf_op jit(solution)/shard_map/all_gather | solution.py:32
  318.0 5.8 fusion.34
  323.9 0.1 convert_reduce_fusion
  324.0 73.1 %reduce-scatter.5.cloned.1.call-done = f32[64,512]{1,0:T(8,128)} async-done(((f32[1024,512]{1,0:T(8,128)}), f32[64,512]{1,0:T(8,128)}) %reduce-scatter.5.cloned.1.call-update) | async-done | bytes 131088 | tf_op jit(solution)/shard_map/reduce_scatter | solution.py:36
  397.0 0.9 reduce_sum.37
  398.0 31.4 %psum.42 = f32[512]{0:T(512)S(1)} all-reduce(f32[512]{0:T(512)S(1)} %reduce_sum.37), channel_id=1, replica_groups=mesh['dp'=16,'tensor'=16] {'tensor'}, use_global_device_ids=true, to_apply=%region_3.4 | all-reduce | flops 512 | bytes 4096 | tf_op jit(solution)/shard_map/psum | solution.py:39
  429.3 0.9 multiply_reduce_fusion
  430.3 32.0 %all-reduce.1 = (f32[256]{0:T(256)S(1)}, f32[512]{0:T(512)S(1)}) all-reduce(f32[256]{0:T(256)S(1)} %convert_reduce_fusion, f32[512]{0:T(512)S(1)} %multiply_reduce_fusion), channel_id=1, replica_groups=mesh['dp'=16,'tensor'=16] {'tensor'}, use_global_device_ids=true, to_apply=%region_5.6 | all-reduce | flops 768 | bytes 6144 | tf_op jit(solution)/shard_map/psum | solution.py:39
  462.3 2.4 fusion.10
  464.7 0.2 all-reduce.8.cloned.1.call-start
  464.9 173.9 %all-reduce.6.cloned.1.call-done = f32[512,256]{1,0:T(8,128)} async-done(((f32[512,256]{1,0:T(8,128)}), f32[512,256]{1,0:T(8,128)}) %all-reduce.6.cloned.1.call-update) | async-done | bytes 524304 | tf_op jit(solution)/shard_map/psum | solution.py:44
  638.8 2.2 fusion.7
  641.1 3.1 fusion.32
  644.2 182.0 %all-reduce.8.cloned.1.call-done = (f32[256,256]{0,1:T(8,128)}, f32[256,64]{0,1:T(8,128)}) async-done(((f32[256,256]{0,1:T(8,128)}, f32[256,64]{0,1:T(8,128)}), (f32[256,256]{0,1:T(8,128)}, f32[256,64]{0,1:T(8,128)})) %all-reduce.8.cloned.1.call-update) | async-done | bytes 327696 | tf_op jit(solution)/shard_map/psum | solution.py:50
  826.2 1.6 select_reduce_fusion
  828.5 1.0 select_add_fusion
  829.5 0.1 copy.28
  829.6 1.0 fusion.6
  830.6 11.7 %cholesky.49 = f32[128,128]{1,0:T(8,128)S(1)} custom-call(f32[128,128]{1,0:T(8,128)S(1)} %cholesky.115), custom_call_target="Cholesky" | custom-call | tf_op jit(solution)/shard_map/jit(cholesky)/cholesky | solution.py:58
  842.4 9.8 %custom-call.18 = f32[1,128,128]{1,2,0:T(8,128)S(1)} custom-call(f32[1,128,128]{2,1,0:T(8,128)S(1)} %get-tuple-element.44), custom_call_target="InvertDiagBlocksLowerTriangular" | custom-call | tf_op jit(solution)/shard_map/jit(cholesky)/cholesky | solution.py:58
  852.2 0.2 fusion.12
  852.4 0.3 convolution_subtract_fusion
  852.6 11.7 %cholesky.103 = f32[128,128]{1,0:T(8,128)S(1)} custom-call(f32[128,128]{1,0:T(8,128)S(1)} %convolution_subtract_fusion), custom_call_target="Cholesky" | custom-call | tf_op jit(solution)/shard_map/jit(cholesky)/cholesky | solution.py:58
  864.4 0.1 copy.31
  864.5 0.1 copy.30
  864.6 0.1 copy.29
  864.7 0.7 compare_reduce_fusion
  866.9 4.3 while.1
  866.9 0.6 fusion.46
  867.5 1.4 dynamic-slice.7
  869.0 0.1 copy.38
  869.1 0.6 fusion.46
  869.7 1.4 dynamic-slice.7
  871.3 19.7 %custom-call.19 = f32[2,128,128]{1,2,0:T(8,128)S(1)} custom-call(f32[2,128,128]{2,1,0:T(8,128)S(1)} %get-tuple-element.12), custom_call_target="InvertDiagBlocksLowerTriangular" | custom-call | tf_op jit(solution)/shard_map/jit(_cho_solve)/triangular_solve | solution.py:59
  891.0 0.2 fusion.22
  891.2 0.2 convolution_subtract_fusion.2
  891.3 0.2 fusion.24
  891.5 0.2 fusion.23
  891.8 0.2 convolution_subtract_fusion.1
  892.0 0.2 fusion.21
  892.3 1.3 fusion.4
  (38 shorter events, 0.6 us)
Async XLA Ops:
  6.5 311.5 %copy-start = (bf16[1848,512]{1,0:T(8,128)(2,1)S(1)}, bf16[1848,512]{1,0:T(8,128)(2,1)}, u32[]{:S(2)}) copy-start(bf16[1848,512]{1,0:T(8,128)(2,1)} %param.8) | copy-start | bytes 5677060
  6.5 77.2 %all-gather.3.cloned.1.call-start = ((), (), s32[]{:S(2)}) async-start(), calls=%async_computation.2 | async-start | bytes 1114112 | tf_op jit(solution)/shard_map/all_gather | solution.py:19
  7.3 234.8 %reduce-scatter.7.cloned.1.call-start = ((), (), s32[]{:S(2)}) async-start(), calls=%async_computation.6 | async-start | bytes 8077312 | tf_op jit(solution)/shard_map/reduce_scatter | solution.py:24
  103.6 214.4 %all-gather.5.cloned.1.call-start = ((), (), s32[]{:S(2)}) async-start(), calls=%async_computation.3 | async-start | bytes 4177920 | tf_op jit(solution)/shard_map/all_gather | solution.py:32
  244.1 79.8 %copy-start.3 = (s32[64]{0:T(128)S(1)}, s32[64]{0:T(128)}, u32[]{:S(2)}) copy-start(s32[64]{0:T(128)} %param.9) | copy-start | bytes 772
  244.1 152.9 %reduce-scatter.5.cloned.1.call-start = ((), (), s32[]{:S(2)}) async-start(), calls=%async_computation.4 | async-start | bytes 2228224 | tf_op jit(solution)/shard_map/reduce_scatter | solution.py:36
  323.8 315.0 %all-reduce.6.cloned.1.call-start = ((), (), s32[]{:S(2)}) async-start(), calls=%async_computation.5 | async-start | bytes 1048576 | tf_op jit(solution)/shard_map/psum | solution.py:44
  464.7 361.5 %all-reduce.8.cloned.1.call-start = ((), (), s32[]{:S(2)}) async-start(), calls=%async_computation.7 | async-start | bytes 655360 | tf_op jit(solution)/shard_map/psum | solution.py:50
  644.2 248.1 %copy-start.1 = (f32[64,512]{1,0:T(8,128)S(1)}, f32[64,512]{1,0:T(8,128)}, u32[]{:S(2)}) copy-start(f32[64,512]{1,0:T(8,128)} %reduce-scatter.5.cloned.1.call-done) | copy-start | bytes 393220
  644.2 248.1 %copy-start.4 = (f32[512,256]{1,0:T(8,128)S(1)}, f32[512,256]{1,0:T(8,128)}, u32[]{:S(2)}) copy-start(f32[512,256]{1,0:T(8,128)} %all-reduce.6.cloned.1.call-done) | copy-start | bytes 1572868
  826.2 64.8 %copy-start.2 = (f32[256,64]{0,1:T(8,128)S(1)}, f32[256,64]{0,1:T(8,128)}, u32[]{:S(2)}) copy-start(f32[256,64]{0,1:T(8,128)} %get-tuple-element.40) | copy-start | bytes 196612
Sparse Core Ops, SparseCore 0:
  9.1 74.5 all-gather.2
  103.7 138.3 reduce-scatter.6
  245.1 72.8 all-gather.4
  323.9 73.0 reduce-scatter.4
  464.8 173.9 all-reduce.5
  644.3 181.8 all-reduce.7
where the time goes:
time: 901 us; the launch traced here: 900 us
  waiting for transfers between devices  718 us (80%)
  blocking collectives  63.4 us (7%)
  other arithmetic  61.3 us (7%)
  matrix products  26.1 us (3%)
  between operations  15.7 us (2%)
  local copies, waits for them, and re-layouts  15.1 us (2%)
    psum x1, waiting for transfers between devices, shards(): lax.psum((jnp.dot(whitened.T, whitened, precision=high), jnp.dot(white_ro...  182 us
    psum x1, waiting for transfers between devices, shards(): lax.psum((cross_part, jnp.sum(centred * centred, axis=0)), 'tensor')  174 us
    reduce_scatter x1, waiting for transfers between devices, shards(): lax.psum_scatter(lax.optimization_barrier(partial_value).astype(jnp.float...  138 us
    all_gather x1, waiting for transfers between devices, shards(): gathered = lax.all_gather(tokens, 'tensor', axis=0, tiled=True)  76.4 us
    all_gather x1, waiting for transfers between devices, shards(): lax.all_gather(hidden, 'dp', axis=0, tiled=True)  73.9 us
    reduce_scatter x1, waiting for transfers between devices, shards(): lax.psum_scatter(partial_out, 'tensor', scatter_dimension=0, tiled=True)  73.1 us
    psum x2, blocking collectives, shards(): lax.psum((jnp.sum(output, axis=0), jnp.sum(onehot, axis=0)), 'tensor')  63.4 us
    another operation x6, other arithmetic, shards(): jnp.linalg.cholesky(gram_mat + ridge_term * jnp.eye(NCLS, dtype=jnp.float...  34 us
  transfers between devices with their start and end apart: 6, of which 6 were waited for; matrix products, arithmetic and copies ran while one was open for 0% of the time, Pallas kernels for 0%

commit v1 on v0

v1 whole, which is shorter than its diff:
```python
import functools

import jax
import jax.numpy as jnp
from jax import lax
from jax.experimental import pallas as pl
from jax.experimental.pallas import tpu as pltpu
from jax.sharding import PartitionSpec as P

MESH = pl.DeviceIdType.MESH
NCLS = 256
TOKENS = 1024
UNITS = 928
SHIFT = 920
CHUNKS = (240, 240, 224, 224)
epsilon = 1e-05
ridge_share = 0.5
f32 = jnp.float32
bf16 = jnp.bfloat16
VM = pl.BlockSpec(memory_space=pltpu.VMEM)
ANY = pl.BlockSpec(memory_space=pl.ANY)


class Spot:
    def __init__(self):
        dp, tn = lax.axis_index("dp"), lax.axis_index("tensor")
        self.dp, self.tn = dp, tn
        self.core = lax.rem(dp, 2)
        self.zh = lax.rem(dp // 2, 2)
        self.y = dp // 4
        self.x = lax.rem(tn, 4)
        self.zl = tn // 4

    def dpid(self, y=None, zh=None, core=None):
        y = self.y if y is None else y
        zh = self.zh if zh is None else zh
        core = self.core if core is None else core
        return {"dp": y * 4 + zh * 2 + core}

    def tid(self, zl=None, x=None):
        zl = self.zl if zl is None else zl
        x = self.x if x is None else x
        return {"tensor": zl * 4 + x}


def up4(v, d):
    return lax.rem(v + d, 4)


def greet(peers):
    barrier = pltpu.get_barrier_semaphore()
    for peer in peers:
        pl.semaphore_signal(barrier, inc=1, device_id=peer, device_id_type=MESH)
    pl.semaphore_wait(barrier, len(peers))


def push(src, dst, ssem, rsem, dev):
    copy = pltpu.make_async_remote_copy(
        src_ref=src, dst_ref=dst, send_sem=ssem, recv_sem=rsem, device_id=dev, device_id_type=MESH
    )
    copy.start()
    return copy


def gather_tensor(me, parts):
    copies = []
    zc, rc, lc, fc = {}, {}, {}, {}
    right, left = up4(me.x, 1), up4(me.x, 3)
    for i, (own, block, ss, rs) in enumerate(parts):
        for d in (1, 2, 3):
            zc[i, d] = push(own, block(me.zl, me.x), ss.at[d], rs.at[d], me.tid(zl=up4(me.zl, d)))
    for d in range(4):
        z = up4(me.zl, 4 - d)
        for i, (own, block, ss, rs) in enumerate(parts):
            src = own
            if d:
                zc[i, d].wait_recv()
                src = block(z, me.x)
            rc[i, d] = push(src, block(z, me.x), ss.at[4 + d], rs.at[4 + d], me.tid(x=right))
            lc[i, d] = push(src, block(z, me.x), ss.at[8 + d], rs.at[8 + d], me.tid(x=left))
    for d in range(4):
        z = up4(me.zl, 4 - d)
        for i, (own, block, ss, rs) in enumerate(parts):
            rc[i, d].wait_recv()
            lc[i, d].wait_recv()
            if d < 2:
                v = block(z, left)
                fc[i, d] = push(v, v, ss.at[12 + d], rs.at[12 + d], me.tid(x=right))
            else:
                v = block(z, right)
                fc[i, d] = push(v, v, ss.at[12 + d], rs.at[12 + d], me.tid(x=left))
    for c in fc.values():
        c.wait_recv()
    return [*zc.values(), *rc.values(), *lc.values(), *fc.values()]


def tensor_peers(me):
    peers = [me.tid(zl=up4(me.zl, d)) for d in (1, 2, 3)]
    return peers + [me.tid(x=up4(me.x, 1)), me.tid(x=up4(me.x, 3))]


def nt(a, b):
    return lax.dot_general(a, b, (((1,), (1,)), ((), ())), preferred_element_type=f32)


def hidden_kernel(tok, lab, wg, wu, h, labs, T, Tp, W, S, R, K2, PO, SZ, RZ,
                  ts, tr, ls, lr, ws, wr, wl, cs, cr, rs, rr, zs, zr):
    me = Spot()
    other = 1 - me.core
    own_rows = pl.ds(pl.multiple_of(SHIFT * me.core, 8), UNITS)
    far_rows = pl.ds(pl.multiple_of(SHIFT * other, 8), UNITS)
    local = []
    for i, w in enumerate((wg, wu)):
        c = pltpu.make_async_copy(w.at[own_rows], W.at[0, i], wl.at[i])
        c.start()
        local.append(c)
    yr, yl = up4(me.y, 1), up4(me.y, 3)
    to_r, to_l = me.dpid(y=yr), me.dpid(y=yl)
    mate = me.dpid(core=other)
    greet(tensor_peers(me) + [to_r, to_l, me.dpid(zh=1 - me.zh), mate])
    sent = []
    wx = []
    for i, w in enumerate((wg, wu)):
        wx.append(push(w.at[far_rows], W.at[1, i], ws.at[i], wr.at[i], mate))

    def tblock(zl, x):
        return T.at[pl.ds(pl.multiple_of(64 * (4 * zl + x), 64), 64)]

    def lblock(zl, x):
        return labs.at[4 * zl + x]

    T[pl.ds(pl.multiple_of(64 * me.tn, 64), 64), :] = tok[...]
    labs[me.tn] = lab[...]
    sent += gather_tensor(me, [(tok, tblock, ts, tr), (lab, lblock, ls, lr)])
    order = (2, 1, 3, 0)
    tx = []
    for k, d in enumerate(order):
        rows = pl.ds(pl.multiple_of(256 * up4(me.y, d), 256), 256)
        tx.append(push(T.at[rows], Tp.at[rows], cs.at[k], cr.at[k], mate))
    for c in local:
        c.wait()
    for c in wx:
        c.wait_recv()
    for c in tx:
        c.wait_recv()
    sent += wx + tx

    starts = [sum(CHUNKS[:q]) for q in range(len(CHUNKS))]

    def mult(i, q, d):
        a, n = starts[q], CHUNKS[q]
        rows = pl.ds(pl.multiple_of(256 * up4(me.y, d), 256), 256)
        return nt(W[0, i, a:a + n, :], T[rows, :]) + nt(W[1, i, a:a + n, :], Tp[rows, :])

    cps = {}

    def send(k, q, dev):
        rows = pl.ds(2 * starts[q], 2 * CHUNKS[q])
        cps[k, q] = push(S.at[k, rows], R.at[k, rows], rs.at[k, q], rr.at[k, q], dev)

    def first(q):
        a, n = starts[q], CHUNKS[q]
        for i in range(2):
            o = 2 * a + i * n
            p = mult(i, q, 2)
            S[0, o:o + n, :] = p[:, :128].astype(bf16)
            S[1, o:o + n, :] = p[:, 128:].astype(bf16)
        send(0, q, to_r)
        send(1, q, to_l)
        for i in range(2):
            o = 2 * a + i * n
            p = mult(i, q, 1)
            K2[0, o:o + n, :] = p[:, :128]
            S[3, o:o + n, :] = p[:, 128:].astype(bf16)
        send(3, q, to_r)
        for i in range(2):
            o = 2 * a + i * n
            p = mult(i, q, 3)
            K2[1, o:o + n, :] = p[:, 128:]
            S[4, o:o + n, :] = p[:, :128].astype(bf16)
        send(4, q, to_l)
        for i in range(2):
            o = 2 * a + i * n
            PO[o:o + n, :] = mult(i, q, 0)

    def second(q):
        o, n = 2 * starts[q], 2 * CHUNKS[q]
        cps[0, q].wait_recv()
        S[2, o:o + n, :] = (K2[0, o:o + n, :] + R[0, o:o + n, :].astype(f32)).astype(bf16)
        send(2, q, to_r)
        cps[1, q].wait_recv()
        S[5, o:o + n, :] = (K2[1, o:o + n, :] + R[1, o:o + n, :].astype(f32)).astype(bf16)
        send(5, q, to_l)

    zc = {}

    def third(q):
        o, n = 2 * starts[q], 2 * CHUNKS[q]
        for k in (2, 3, 4, 5):
            cps[k, q].wait_recv()
        a = PO[o:o + n, :128] + R[2, o:o + n, :].astype(f32) + R[4, o:o + n, :].astype(f32)
        b = PO[o:o + n, 128:] + R[3, o:o + n, :].astype(f32) + R[5, o:o + n, :].astype(f32)
        low = me.zh == 0
        SZ[o:o + n, :] = jnp.where(low, b, a).astype(bf16)
        PO[o:o + n, :128] = jnp.where(low, a, b)
        rows = pl.ds(o, n)
        zc[q] = push(SZ.at[rows], RZ.at[rows], zs.at[q], zr.at[q], me.dpid(zh=1 - me.zh))

    def last(q):
        a, n = starts[q], CHUNKS[q]
        o = 2 * a
        zc[q].wait_recv()
        tot = PO[o:o + 2 * n, :128] + RZ[o:o + 2 * n, :].astype(f32)
        g, u = tot[:n], tot[n:]
        h[a:a + n, :] = (g / (1.0 + jnp.exp(-g)) * u).astype(bf16)

    nq = len(CHUNKS)
    for i in range(nq + 2):
        if i < nq:
            first(i)
        if 1 <= i <= nq:
            second(i - 1)
        if i >= 2:
            third(i - 2)
    for q in range(nq):
        last(q)
    for c in [*sent, *cps.values(), *zc.values()]:
        c.wait_send()


def down_kernel(h, down, outt, D, DT, H, PG, KO, SO, RO, SZ, RZ,
                dl, hs, hr, cs, cr, os, orr, zs, zr):
    me = Spot()
    other = 1 - me.core
    loads = []
    for i, c in enumerate((me.core, other)):
        cp = pltpu.make_async_copy(
            down.at[pl.ds(pl.multiple_of(SHIFT * c, 8), UNITS)], D.at[i, pl.ds(0, UNITS)], dl.at[i]
        )
        cp.start()
        loads.append(cp)
    yr, yl, yf = up4(me.y, 1), up4(me.y, 3), up4(me.y, 2)
    to_r, to_l = me.dpid(y=yr), me.dpid(y=yl)
    mate = me.dpid(core=other)
    across = me.dpid(zh=1 - me.zh)
    xr, xl = me.tid(x=up4(me.x, 1)), me.tid(x=up4(me.x, 3))
    greet(tensor_peers(me) + [to_r, to_l, across, mate])

    def hv(i, y, zh):
        return H.at[i, y, pl.ds(0, UNITS), pl.ds(pl.multiple_of(128 * zh, 128), 128)]

    zh, zo = me.zh, 1 - me.zh
    sent = []
    cc = {}

    def share(k, src, y, z):
        cc[k] = push(src, hv(1, y, z), cs.at[k], cr.at[k], mate)
        sent.append(cc[k])

    cz = push(h, hv(0, me.y, zh), hs.at[0], hr.at[0], across)
    cr0 = push(h, hv(0, me.y, zh), hs.at[1], hr.at[1], to_r)
    cl0 = push(h, hv(0, me.y, zh), hs.at[2], hr.at[2], to_l)
    share(0, h, me.y, zh)
    H[0, me.y, 0:UNITS, pl.ds(pl.multiple_of(128 * zh, 128), 128)] = h[...]
    H[:, :, UNITS:, :] = jnp.zeros((2, 4, 1024 - UNITS, 256), bf16)
    for i in range(2):
        loads[i].wait()
        D[i, UNITS:, :] = jnp.zeros((1024 - UNITS, 512), bf16)
        dup = (me.core if i == 0 else other) == 1
        head = D[i, 0:16, :].astype(f32)
        row = lax.broadcasted_iota(jnp.int32, head.shape, 0)
        D[i, 0:16, :] = jnp.where(jnp.logical_and(dup, row < 8), 0.0, head).astype(bf16)
        for k in range(4):
            DT[i, :, 256 * k:256 * k + 256] = D[i, 256 * k:256 * k + 256, :].T
    cz.wait_recv()
    v = hv(0, me.y, zo)
    cr1 = push(v, v, hs.at[3], hr.at[3], to_r)
    cl1 = push(v, v, hs.at[4], hr.at[4], to_l)
    share(1, v, me.y, zo)
    cr0.wait_recv()
    v = hv(0, yl, zh)
    fr = push(v, v, hs.at[5], hr.at[5], to_r)
    share(2, v, yl, zh)
    cl0.wait_recv()
    share(3, hv(0, yr, zh), yr, zh)

    oc = {}

    def osend(g, k, dev):
        oc[g, k] = push(SO.at[g, k], RO.at[g, k], os.at[g, k], orr.at[g, k], dev)

    def rows(d):
        return pl.ds(pl.multiple_of(128 * up4(me.x, d), 128), 128)

    def group(g, y):
        PG[...] = jnp.dot(DT[0], H[0, y], preferred_element_type=f32) + jnp.dot(
            DT[1], H[1, y], preferred_element_type=f32
        )
        SO[g, 0] = PG[rows(2), 0:128].astype(bf16)
        SO[g, 1] = PG[rows(2), 128:256].astype(bf16)
        osend(g, 0, xr)
        osend(g, 1, xl)
        SO[g, 3] = PG[rows(1), 128:256].astype(bf16)
        osend(g, 3, xr)
        SO[g, 4] = PG[rows(3), 0:128].astype(bf16)
        osend(g, 4, xl)
        KO[g, 0] = PG[rows(1), 0:128]
        KO[g, 1] = PG[rows(3), 128:256]
        KO[g, 2] = PG[rows(0), 0:128]
        KO[g, 3] = PG[rows(0), 128:256]

    def relay(g):
        oc[g, 0].wait_recv()
        SO[g, 2] = (KO[g, 0] + RO[g, 0].astype(f32)).astype(bf16)
        osend(g, 2, xr)
        oc[g, 1].wait_recv()
        SO[g, 5] = (KO[g, 1] + RO[g, 1].astype(f32)).astype(bf16)
        osend(g, 5, xl)

    zc = {}

    def settle(g):
        for k in (2, 3, 4, 5):
            oc[g, k].wait_recv()
        KO[g, 2] = KO[g, 2] + RO[g, 2].astype(f32) + RO[g, 4].astype(f32)
        KO[g, 3] = KO[g, 3] + RO[g, 3].astype(f32) + RO[g, 5].astype(f32)
        SZ[g, 0] = KO[g, 2].astype(bf16)
        SZ[g, 1] = KO[g, 3].astype(bf16)
        for d in (1, 2, 3):
            z = up4(me.zl, d)
            part = pl.ds(pl.multiple_of(32 * z, 32), 32)
            zc[g, d] = push(
                SZ.at[g, pl.ds(0, 2), part], RZ.at[g, d - 1], zs.at[g, d - 1], zr.at[g, d - 1], me.tid(zl=z)
            )

    def close(g, y):
        mine = pl.ds(pl.multiple_of(32 * me.zl, 32), 32)
        for d in (1, 2, 3):
            zc[g, d].wait_recv()
        for b in range(2):
            tot = KO[g, 2 + b, mine, :]
            for d in range(3):
                tot = tot + RZ[g, d, b].astype(f32)
            outt[:, pl.ds(pl.multiple_of(256 * y + 128 * b, 128), 128)] = tot

    cc[0].wait_recv()
    cc[1].wait_recv()
    group(0, me.y)
    cl1.wait_recv()
    v = hv(0, yr, zo)
    fl = push(v, v, hs.at[6], hr.at[6], to_l)
    share(4, v, yr, zo)
    cr1.wait_recv()
    share(5, hv(0, yl, zo), yl, zo)
    cc[3].wait_recv()
    cc[4].wait_recv()
    group(1, yr)
    relay(0)
    cc[2].wait_recv()
    cc[5].wait_recv()
    group(2, yl)
    relay(1)
    fr.wait_recv()
    share(6, hv(0, yf, zh), yf, zh)
    settle(0)
    fl.wait_recv()
    share(7, hv(0, yf, zo), yf, zo)
    cc[6].wait_recv()
    cc[7].wait_recv()
    group(3, yf)
    relay(2)
    settle(1)
    relay(3)
    settle(2)
    close(0, me.y)
    settle(3)
    close(1, yr)
    close(2, yl)
    close(3, yf)
    for c in [*sent, cz, cr0, cl0, cr1, cl1, fr, fl, *oc.values(), *zc.values()]:
        c.wait_send()


def stats_kernel(outt, labs, gram, coords, wall, zall, ms,
                 zb, zg, X, XR, XS, XA, XF, GB,
                 ws, wr, ms_s, ms_r, as_, ar, xs, xr, gs, gr):
    me = Spot()
    other = 1 - me.core
    mate = me.dpid(core=other)
    chips = [(dy, dz) for dy in range(4) for dz in range(2) if dy or dz]
    chip_dev = [me.dpid(y=up4(me.y, dy), zh=lax.rem(me.zh + dz, 2)) for dy, dz in chips]
    t_dev = [{"tensor": lax.rem(me.tn + d, 16)} for d in range(1, 16)]
    greet(t_dev + chip_dev + [mate])

    out = outt[...]
    mean = jnp.sum(out, axis=1, keepdims=True) / TOKENS
    cen = out - mean
    spread = jnp.sqrt(jnp.sum(cen * cen, axis=1, keepdims=True) / TOKENS + epsilon)
    z = cen / spread
    for j in range(8):
        zb[j] = z[:, 128 * j:128 * j + 128].astype(bf16)
    slot = 4 * me.x + me.zl

    def rows32(zl, x):
        return pl.ds(pl.multiple_of(32 * (4 * x + zl), 32), 32)

    ac = []
    for d in range(1, 16):
        t = lax.rem(me.tn + d, 16)
        ac.append(push(zb.at[t // 2], zg.at[rows32(me.zl, me.x)], as_.at[d - 1], ar.at[d - 1], t_dev[d - 1]))
    zg[rows32(me.zl, me.x), :] = zb[me.tn // 2]

    cls = lax.broadcasted_iota(jnp.int32, (NCLS, 128), 0)
    c1 = cen.astype(bf16)
    r1 = cen - c1.astype(f32)
    c2 = r1.astype(bf16)
    c3 = (r1 - c2.astype(f32)).astype(bf16)
    acc = jnp.zeros((32, NCLS), f32)
    for j in range(8):
        row = labs[2 * j, 0:1, :] + labs[2 * j + 1, 0:1, :]
        hot = (cls == row).astype(f32).astype(bf16)
        cols = slice(128 * j, 128 * j + 128)
        acc = acc + nt(c1[:, cols], hot) + nt(c2[:, cols], hot) + nt(c3[:, cols], hot)
    wall[rows32(me.zl, me.x), :] = (acc / TOKENS / spread).astype(bf16)
    lane = lax.broadcasted_iota(jnp.int32, (32, 128), 1)
    ms[rows32(me.zl, me.x), :] = jnp.where(lane < 64, mean, spread)

    def wv(zl, x):
        return wall.at[rows32(zl, x)]

    def mv(zl, x):
        return ms.at[rows32(zl, x)]

    sent = gather_tensor(
        me, [(wv(me.zl, me.x), wv, ws, wr), (mv(me.zl, me.x), mv, ms_s, ms_r)]
    )
    for c in ac:
        c.wait_recv()
    sent += ac
    zz = zg[...].astype(f32)
    zz = jnp.where(lax.rem(me.tn, 2) == 1, pltpu.roll(zz, 64, 1), zz)
    zall[...] = zz.astype(bf16)
    wt = wall[...].T
    G = jnp.dot(wt, wall[...], preferred_element_type=f32)
    C = jnp.dot(wt, zall[...], preferred_element_type=f32)
    gram[...] = G
    lane = lax.broadcasted_iota(jnp.int32, (128, 128), 1)
    X[0:128, :] = jnp.where(lane < 64, C[:128], pltpu.roll(C[128:], 64, 1))
    mine = pl.ds(pl.multiple_of(16 * me.tn, 16), 16)
    X[128:144, :] = gram[mine, 0:128]
    X[144:160, :] = gram[mine, 128:256]
    half = lambda c: pl.ds(pl.multiple_of(80 * c, 8), 80)
    c0 = push(X.at[half(other)], XR, xs.at[0], xr.at[0], mate)
    c0.wait_recv()
    chip = me.y * 2 + me.zh
    XS[...] = X[half(me.core), :] + XR[...]
    XA[chip] = XS[...]
    xc = []
    for k, dev in enumerate(chip_dev):
        xc.append(push(XS, XA.at[chip], xs.at[1 + k], xr.at[1 + k], dev))
    for c in xc:
        c.wait_recv()
    tot = XA[0]
    for k in range(1, 8):
        tot = tot + XA[k]
    XF[half(me.core), :] = tot
    c1x = push(XF.at[half(me.core)], XF.at[half(me.core)], xs.at[8], xr.at[8], mate)
    c1x.wait_recv()
    GB[me.tn] = XF[128:160, :]

    def gv(zl, x):
        return GB.at[4 * zl + x]

    sent += gather_tensor(me, [(gv(me.zl, me.x), gv, gs, gr)])
    for t in range(16):
        gram[16 * t:16 * t + 16, 0:128] = GB[t, 0:16, :]
        gram[16 * t:16 * t + 16, 128:256] = GB[t, 16:32, :]
    coords[0:128, :] = XF[0:128, :]
    coords[128:256, :] = pltpu.roll(XF[0:128, :], 64, 1)
    for c in [*sent, c0, *xc, c1x]:
        c.wait_send()


def params(cid):
    return pltpu.CompilerParams(collective_id=cid, has_side_effects=True, vmem_limit_bytes=56 * 2**20)


DMA = pltpu.SemaphoreType.DMA
V = pltpu.VMEM
S = jax.ShapeDtypeStruct


def shards(tokens, gate_weight, up_weight, down_weight, labels):
    tn = lax.axis_index("tensor")
    twice = jnp.concatenate([labels, labels])[None, :]
    keep = (jnp.arange(128) // 64)[None, :] == tn % 2
    lab = jnp.broadcast_to(jnp.where(keep, twice, 0), (8, 128))
    nq = len(CHUNKS)
    h, labs = pl.pallas_call(
        hidden_kernel,
        out_shape=(S((UNITS, 128), bf16), S((16, 8, 128), jnp.int32)),
        in_specs=[VM, VM, ANY, ANY],
        out_specs=(VM, VM),
        scratch_shapes=[
            V((1024, 512), bf16), V((1024, 512), bf16), V((2, 2, UNITS, 512), bf16),
            V((6, 2 * UNITS, 128), bf16), V((6, 2 * UNITS, 128), bf16), V((2, 2 * UNITS, 128), f32),
            V((2 * UNITS, 256), f32), V((2 * UNITS, 128), bf16), V((2 * UNITS, 128), bf16),
            DMA((16,)), DMA((16,)), DMA((16,)), DMA((16,)), DMA((2,)), DMA((2,)), DMA((2,)),
            DMA((4,)), DMA((4,)), DMA((6, nq)), DMA((6, nq)), DMA((nq,)), DMA((nq,)),
        ],
        compiler_params=params(0),
        name="gate_up_hidden",
    )(tokens, lab, gate_weight.T, up_weight.T)
    outt = pl.pallas_call(
        down_kernel,
        out_shape=S((32, 1024), f32),
        in_specs=[VM, ANY],
        out_specs=VM,
        scratch_shapes=[
            V((2, 1024, 512), bf16), V((2, 512, 1024), bf16), V((2, 4, 1024, 256), bf16),
            V((512, 256), f32), V((4, 4, 128, 128), f32), V((4, 6, 128, 128), bf16),
            V((4, 6, 128, 128), bf16), V((4, 2, 128, 128), bf16), V((4, 3, 2, 32, 128), bf16),
            DMA((2,)), DMA((7,)), DMA((7,)), DMA((8,)), DMA((8,)),
            DMA((4, 6)), DMA((4, 6)), DMA((4, 3)), DMA((4, 3)),
        ],
        compiler_params=params(1),
        name="down_scatter",
    )(h, down_weight)
    gram_mat, coords, wall, zall, ms = pl.pallas_call(
        stats_kernel,
        out_shape=(S((256, 256), f32), S((256, 128), f32), S((512, 256), bf16), S((512, 128), bf16), S((512, 128), f32)),
        in_specs=[VM, VM],
        out_specs=(VM, VM, VM, VM, VM),
        scratch_shapes=[
            V((8, 32, 128), bf16), V((512, 128), bf16), V((160, 128), f32), V((80, 128), f32),
            V((80, 128), f32), V((8, 80, 128), f32), V((160, 128), f32), V((16, 32, 128), f32),
            DMA((16,)), DMA((16,)), DMA((16,)), DMA((16,)), DMA((15,)), DMA((15,)),
            DMA((9,)), DMA((9,)), DMA((16,)), DMA((16,)),
        ],
        compiler_params=params(2),
        name="stats_gram",
    )(outt, labs)
    ridge_term = ridge_share * jnp.trace(gram_mat) / NCLS
    factor = jnp.linalg.cholesky(gram_mat + ridge_term * jnp.eye(NCLS, dtype=f32))
    solved = jax.scipy.linalg.cho_solve((factor, True), coords[:, :64])
    fix = jnp.dot(wall, solved.astype(bf16), preferred_element_type=f32)
    erased = ms[:, 0:1] + ms[:, 64:65] * (zall[:, :64].astype(f32) - fix)
    return erased.T.astype(bf16)


def solution(mesh):
    return jax.shard_map(
        shards,
        mesh=mesh,
        in_specs=(
            P("tensor", "dp"),
            P("dp", "tensor"),
            P("dp", "tensor"),
            P("tensor", "dp"),
            P("tensor"),
        ),
        out_specs=P("tensor", "dp"),
        check_vma=False,
    )
```

time: 901 us -> 231 us (0.26)
  waiting for transfers between devices: 718 us -> 0 us
  Pallas kernels: 0 us -> 160 us
  blocking collectives: 63.4 us -> 0 us
  matrix products: 26.1 us -> 2.25 us
  between operations: 15.7 us -> 2.26 us
    psum x2 -> x0, waiting for transfers between devices: 356 us -> none  [the longest x1 182 us: shards(): lax.psum((jnp.dot(whitened.T, whitened, precision=high), jnp.dot(white_ro...]
    reduce_scatter x2 -> x0, waiting for transfers between devices: 211 us -> none  [the longest x1 138 us: shards(): lax.psum_scatter(lax.optimization_barrier(partial_value).astype(jnp.float...]
    pallas_call x0 -> x3, Pallas kernels: none -> 160 us  [the longest x1 71.7 us: shards(): pl.pallas_call(hidden_kernel, out_shape=(S((UNITS, 128), bf16), S((16, 8,...]
    all_gather x2 -> x0, waiting for transfers between devices: 150 us -> none  [the longest x1 76.4 us: shards(): gathered = lax.all_gather(tokens, 'tensor', axis=0, tiled=True)]
    psum x2 -> x0, blocking collectives: 63.4 us -> none  [shards(): lax.psum((jnp.sum(output, axis=0), jnp.sum(onehot, axis=0)), 'tensor')]
    dot_general x6 -> x1, matrix products: 24.3 us -> 0.23 us  [shards(): fix = jnp.dot(wall, solved.astype(bf16), preferred_element_type=f32)]
    unnamed x11 -> x6, local copies, waits for them, and re-layouts: 10.3 us -> 0.01 us
  transfers between devices with their start and end apart: 6 -> 0, of which waited for: 6 -> 0; matrix products, arithmetic and copies ran while one was open for 0% -> 0% of each run, Pallas kernels for 0% -> 0%
where the time goes in v1:
time: 231 us; the launch traced here: 229 us
  Pallas kernels  160 us (69%)
  other arithmetic  55.4 us (24%)
  local copies, waits for them, and re-layouts  8.52 us (4%)
    pallas_call x1, Pallas kernels, shards(): pl.pallas_call(hidden_kernel, out_shape=(S((UNITS, 128), bf16), S((16, 8,...  71.7 us
    pallas_call x1, Pallas kernels, shards(): pl.pallas_call(stats_kernel, out_shape=(S((256, 256), f32), S((256, 128),...  44.4 us
    pallas_call x1, Pallas kernels, shards(): pl.pallas_call(down_kernel, out_shape=S((32, 1024), f32), in_specs=[VM, A...  44.1 us
    another operation x6, other arithmetic, shards(): jnp.linalg.cholesky(gram_mat + ridge_term * jnp.eye(NCLS, dtype=f32))  34.2 us
    another operation x3, other arithmetic, shards(): solved = jax.scipy.linalg.cho_solve((factor, True), coords[:, :64])  19.7 us

profile of v1, /device:TPU:1, one launch (start us, length us, event | category | flops | bytes accessed | tf_op | source)
XLA Modules:
  0.0 228.9 jit_solution(12742659127488474406)
XLA Ops:
  0.0 0.8 compare_select_fusion
  0.8 0.6 broadcast_in_dim.9.lab
  1.4 71.7 %gate_up_hidden.1 = (bf16[928,128]{1,0:T(8,128)(2,1)}, s32[16,8,128]{2,1,0:T(8,128)}) custom-call(bf16[64,512]{1,0:T(8,128)(2,1)} %tok.1, s32[8,128]{1,0:T(8,128)} %broadcast_in_dim.9.lab, bf16[1848,512]{1,0:T(8,128)(2,1)} %bitcast.41, bf16[1848,512]{1,0:T(8,128)(2,1)} %bitcast.42), custom_call_target="tpu_custom_call" | custom-call | tf_op jit(solution)/shard_map/gate_up_hidden/pallas_call | solution.py:499
  73.1 44.1 %down_scatter.1.outt = f32[32,1024]{1,0:T(8,128)} custom-call(bf16[928,128]{1,0:T(8,128)(2,1)} %get-tuple-element.12.h, bf16[1848,512]{1,0:T(8,128)(2,1)} %down.1), custom_call_target="tpu_custom_call" | custom-call | tf_op jit(solution)/shard_map/down_scatter/pallas_call | solution.py:514
  117.3 44.4 %stats_gram.1 = (f32[256,256]{1,0:T(8,128)}, f32[256,128]{1,0:T(8,128)}, bf16[512,256]{1,0:T(8,128)(2,1)}, bf16[512,128]{1,0:T(8,128)(2,1)}, f32[512,128]{1,0:T(8,128)}) custom-call(f32[32,1024]{1,0:T(8,128)} %down_scatter.1.outt, s32[16,8,128]{2,1,0:T(8,128)} %get-tuple-element.13.labs), custom_call_target="tpu_custom_call" | custom-call | tf_op jit(solution)/shard_map/stats_gram/pallas_call | solution.py:529
  161.6 1.3 slice_reduce_fusion
  163.0 1.1 copy.25
  164.1 0.6 select_reduce_fusion
  165.4 0.1 copy.26
  165.6 11.9 %cholesky.49 = f32[128,128]{1,0:T(8,128)S(1)} custom-call(f32[128,128]{1,0:T(8,128)S(1)} %cholesky.115), custom_call_target="Cholesky" | custom-call | tf_op jit(solution)/shard_map/jit(cholesky)/cholesky | solution.py:544
  177.5 0.1 copy.27
  177.6 0.0 copy-start
  177.6 9.8 %custom-call.18 = f32[1,128,128]{1,2,0:T(8,128)S(1)} custom-call(f32[1,128,128]{2,1,0:T(8,128)S(1)} %get-tuple-element.52), custom_call_target="InvertDiagBlocksLowerTriangular" | custom-call | tf_op jit(solution)/shard_map/jit(cholesky)/cholesky | solution.py:544
  187.4 0.2 fusion.5
  187.7 0.1 copy.28
  187.8 0.3 convolution_subtract_fusion.2
  188.0 11.7 %cholesky.103 = f32[128,128]{1,0:T(8,128)S(1)} custom-call(f32[128,128]{1,0:T(8,128)S(1)} %convolution_subtract_fusion.2), custom_call_target="Cholesky" | custom-call | tf_op jit(solution)/shard_map/jit(cholesky)/cholesky | solution.py:544
  199.8 0.1 copy.29
  199.9 0.0 copy-start.1
  199.9 0.0 copy-start.2
  199.9 0.7 compare_reduce_fusion
  202.0 0.1 triangular_solve.71
  202.1 4.5 %while.1 = (s32[]{:T(128)}, f32[256,256]{0,1:T(8,128)S(1)}, s32[2,2]{1,0:T(2,128)S(1)}, f32[2,128,128]{2,1,0:T(8,128)S(1)}, s32[]{:T(128)}) while((s32[]{:T(128)}, f32[256,256]{0,1:T(8,128)S(1)}, s32[2,2]{1,0:T(2,128)S(1)}, f32[2,128,128]{2,1,0:T(8,128)S(1)}, s32[]{:T(128)}) %tuple.26), condition=%wide.while_cond, body=%wide.while_body.sunk | while | flops 2 | bytes 393329 | solution.py:545
  202.3 0.6 fusion.29
  202.9 1.4 dynamic-slice.7
  204.3 0.1 copy.39
  204.5 0.6 fusion.29
  205.1 1.4 dynamic-slice.7
  206.5 0.1 copy.39
  206.6 19.7 %custom-call.19 = f32[2,128,128]{1,2,0:T(8,128)S(1)} custom-call(f32[2,128,128]{2,1,0:T(8,128)S(1)} %get-tuple-element.26), custom_call_target="InvertDiagBlocksLowerTriangular" | custom-call | tf_op jit(solution)/shard_map/jit(_cho_solve)/triangular_solve | solution.py:545
  226.3 0.0 copy-done
  226.3 0.3 fusion.8
  226.6 0.3 convolution_subtract_fusion.1
  226.9 0.3 fusion.11
  227.2 0.2 fusion.19
  227.4 0.2 convolution_subtract_fusion.3
  227.7 0.2 convolution_convert_fusion
  227.9 0.0 copy-done.1
  227.9 0.0 copy-done.2
  227.9 0.2 fusion.3
  228.2 0.7 copy.34
  (15 shorter events, 0.3 us)
Async XLA Ops:
  177.6 48.7 %copy-start = (f32[256,128]{1,0:T(8,128)S(1)}, f32[256,128]{1,0:T(8,128)}, u32[]{:S(2)}) copy-start(f32[256,128]{1,0:T(8,128)} %get-tuple-element.18) | copy-start | bytes 393220
  199.9 28.0 %copy-start.1 = (bf16[512,256]{1,0:T(8,128)(2,1)S(1)}, bf16[512,256]{1,0:T(8,128)(2,1)}, u32[]{:S(2)}) copy-start(bf16[512,256]{1,0:T(8,128)(2,1)} %get-tuple-element.16) | copy-start | bytes 786436
  199.9 28.0 %copy-start.2 = (bf16[512,128]{1,0:T(8,128)(2,1)S(1)}, bf16[512,128]{1,0:T(8,128)(2,1)}, u32[]{:S(2)}) copy-start(bf16[512,128]{1,0:T(8,128)(2,1)} %get-tuple-element.15) | copy-start | bytes 393220

commit v2 on v1

--- a/solution.py
+++ b/solution.py
@@ -381,7 +381,45 @@
         c.wait_send()
 
 
-def stats_kernel(outt, labs, gram, coords, wall, zall, ms,
+def scales():
+    low, out = 1.0 / 513.0, []
+    for _ in range(8):
+        out.append(2.0 / (1.0 + low))
+        low = 4.0 * low / (1.0 + low) ** 2
+    return out
+
+
+def solve(FY, gram, coords):
+    sc = scales()
+    eye = lax.broadcasted_iota(jnp.int32, (NCLS, NCLS), 0) == lax.broadcasted_iota(jnp.int32, (NCLS, NCLS), 1)
+    G = gram[...]
+    diag = jnp.where(eye, G, 0.0)
+    trace = jnp.sum(jnp.sum(diag, axis=1, keepdims=True), axis=0, keepdims=True)
+    ridge = ridge_share * trace / NCLS
+    inv = 1.0 / (513.0 * ridge)
+    FY[:, :NCLS] = jnp.where(eye, 1.0 - sc[0] / 513.0, 0.0) - (sc[0] * inv) * G
+    FY[:, NCLS:] = coords[...]
+
+    def pick(k, vals):
+        out = jnp.float32(vals[0])
+        for i in range(1, len(vals)):
+            out = jnp.where(k == i, jnp.float32(vals[i]), out)
+        return out
+
+    def step(k, carry):
+        now, nxt = pick(k, sc[:7]), pick(k, sc[1:])
+        both = jnp.dot(FY[:, :NCLS], FY[...], precision=lax.Precision.HIGHEST, preferred_element_type=f32)
+        FY[:, NCLS:] = now * (FY[:, NCLS:] + both[:, NCLS:])
+        FY[:, :NCLS] = nxt * both[:, :NCLS] + jnp.where(eye, 1.0 - nxt, 0.0)
+        return carry
+
+    lax.fori_loop(0, 7, step, 0)
+    Y = FY[:, NCLS:]
+    last = jnp.dot(FY[:, :NCLS], Y, precision=lax.Precision.HIGHEST, preferred_element_type=f32)
+    return (sc[7] * inv) * (Y + last)
+
+
+def stats_kernel(outt, labs, erased, gram, coords, wall, ms, FY,
                  zb, zg, X, XR, XS, XA, XF, GB,
                  ws, wr, ms_s, ms_r, as_, ar, xs, xr, gs, gr):
     me = Spot()
@@ -439,10 +477,10 @@
     sent += ac
     zz = zg[...].astype(f32)
     zz = jnp.where(lax.rem(me.tn, 2) == 1, pltpu.roll(zz, 64, 1), zz)
-    zall[...] = zz.astype(bf16)
+    zall = zz.astype(bf16)
     wt = wall[...].T
     G = jnp.dot(wt, wall[...], preferred_element_type=f32)
-    C = jnp.dot(wt, zall[...], preferred_element_type=f32)
+    C = jnp.dot(wt, zall, preferred_element_type=f32)
     gram[...] = G
     lane = lax.broadcasted_iota(jnp.int32, (128, 128), 1)
     X[0:128, :] = jnp.where(lane < 64, C[:128], pltpu.roll(C[128:], 64, 1))
@@ -477,6 +515,10 @@
         gram[16 * t:16 * t + 16, 128:256] = GB[t, 16:32, :]
     coords[0:128, :] = XF[0:128, :]
     coords[128:256, :] = pltpu.roll(XF[0:128, :], 64, 1)
+    solved = solve(FY, gram, coords)
+    fix = jnp.dot(wall[...], solved.astype(bf16), preferred_element_type=f32)
+    done = ms[:, 0:1] + ms[:, 64:65] * (zz - fix)
+    erased[...] = done.T[:64].astype(bf16)
     for c in [*sent, c0, *xc, c1x]:
         c.wait_send()
 
@@ -526,26 +568,21 @@
         compiler_params=params(1),
         name="down_scatter",
     )(h, down_weight)
-    gram_mat, coords, wall, zall, ms = pl.pallas_call(
+    return pl.pallas_call(
         stats_kernel,
-        out_shape=(S((256, 256), f32), S((256, 128), f32), S((512, 256), bf16), S((512, 128), bf16), S((512, 128), f32)),
+        out_shape=S((64, 512), bf16),
         in_specs=[VM, VM],
-        out_specs=(VM, VM, VM, VM, VM),
+        out_specs=VM,
         scratch_shapes=[
+            V((256, 256), f32), V((256, 128), f32), V((512, 256), bf16), V((512, 128), f32), V((256, 384), f32),
             V((8, 32, 128), bf16), V((512, 128), bf16), V((160, 128), f32), V((80, 128), f32),
             V((80, 128), f32), V((8, 80, 128), f32), V((160, 128), f32), V((16, 32, 128), f32),
             DMA((16,)), DMA((16,)), DMA((16,)), DMA((16,)), DMA((15,)), DMA((15,)),
             DMA((9,)), DMA((9,)), DMA((16,)), DMA((16,)),
         ],
         compiler_params=params(2),
-        name="stats_gram",
+        name="stats_solve_erase",
     )(outt, labs)
-    ridge_term = ridge_share * jnp.trace(gram_mat) / NCLS
-    factor = jnp.linalg.cholesky(gram_mat + ridge_term * jnp.eye(NCLS, dtype=f32))
-    solved = jax.scipy.linalg.cho_solve((factor, True), coords[:, :64])
-    fix = jnp.dot(wall, solved.astype(bf16), preferred_element_type=f32)
-    erased = ms[:, 0:1] + ms[:, 64:65] * (zall[:, :64].astype(f32) - fix)
-    return erased.T.astype(bf16)
 
 
 def solution(mesh):

time: 231 us -> 169 us (0.73)
  other arithmetic: 55.4 us -> 0.81 us
  local copies, waits for them, and re-layouts: 8.52 us -> 2.07 us
  Pallas kernels: 160 us -> 165 us
    another operation x9 -> x0, other arithmetic: 53.9 us -> none  [the longest x6 34.2 us: shards(): jnp.linalg.cholesky(gram_mat + ridge_term * jnp.eye(NCLS, dtype=f32))]
    another operation x18 -> x0, local copies, waits for them, and re-layouts: 4.64 us -> none
    pallas_call x1, Pallas kernels: 44.4 us -> 48.7 us  [shards(): pl.pallas_call(stats_kernel, out_shape=S((64, 512), bf16), in_specs=[VM,...]
where the time goes in v2:
time: 169 us; the launch traced here: 168 us
  Pallas kernels  165 us (98%)
  local copies, waits for them, and re-layouts  2.07 us (1%)
    pallas_call x1, Pallas kernels, shards(): pl.pallas_call(hidden_kernel, out_shape=(S((UNITS, 128), bf16), S((16, 8,...  71.8 us
    pallas_call x1, Pallas kernels, shards(): pl.pallas_call(stats_kernel, out_shape=S((64, 512), bf16), in_specs=[VM,...  48.7 us
    pallas_call x1, Pallas kernels, shards(): pl.pallas_call(down_kernel, out_shape=S((32, 1024), f32), in_specs=[VM, A...  44.3 us

profile of v2, /device:TPU:1, one launch (start us, length us, event | category | flops | bytes accessed | tf_op | source)
XLA Modules:
  0.0 167.7 jit_solution(17427525147416121933)
XLA Ops:
  0.0 0.8 compare_select_fusion
  0.8 0.6 broadcast_in_dim.4.lab
  1.4 71.8 %gate_up_hidden.1 = (bf16[928,128]{1,0:T(8,128)(2,1)}, s32[16,8,128]{2,1,0:T(8,128)}) custom-call(bf16[64,512]{1,0:T(8,128)(2,1)} %tok.1, s32[8,128]{1,0:T(8,128)} %broadcast_in_dim.4.lab, bf16[1848,512]{1,0:T(8,128)(2,1)} %bitcast.2, bf16[1848,512]{1,0:T(8,128)(2,1)} %bitcast.3), custom_call_target="tpu_custom_call" | custom-call | tf_op jit(solution)/shard_map/gate_up_hidden/pallas_call | solution.py:541
  73.2 44.3 %down_scatter.1.outt = f32[32,1024]{1,0:T(8,128)} custom-call(bf16[928,128]{1,0:T(8,128)(2,1)} %get-tuple-element.7.h, bf16[1848,512]{1,0:T(8,128)(2,1)} %down.1), custom_call_target="tpu_custom_call" | custom-call | tf_op jit(solution)/shard_map/down_scatter/pallas_call | solution.py:556
  117.5 48.7 %stats_solve_erase.1 = bf16[64,512]{1,0:T(8,128)(2,1)} custom-call(f32[32,1024]{1,0:T(8,128)} %down_scatter.1.outt, s32[16,8,128]{2,1,0:T(8,128)} %get-tuple-element.8.labs), custom_call_target="tpu_custom_call" | custom-call | tf_op jit(solution)/shard_map/stats_solve_erase/pallas_call | solution.py:571
  166.2 1.5 copy.7

commit v3 on v2

--- a/solution.py
+++ b/solution.py
@@ -62,7 +62,7 @@
     return copy
 
 
-def gather_tensor(me, parts):
+def gather_tensor(me, parts, done=None):
     copies = []
     zc, rc, lc, fc = {}, {}, {}, {}
     right, left = up4(me.x, 1), up4(me.x, 3)
@@ -89,8 +89,11 @@
             else:
                 v = block(z, right)
                 fc[i, d] = push(v, v, ss.at[12 + d], rs.at[12 + d], me.tid(x=left))
-    for c in fc.values():
-        c.wait_recv()
+    for d in range(4):
+        for i in range(len(parts)):
+            fc[i, d].wait_recv()
+        if done is not None:
+            done(d)
     return [*zc.values(), *rc.values(), *lc.values(), *fc.values()]
 
 
@@ -131,19 +134,27 @@
 
     T[pl.ds(pl.multiple_of(64 * me.tn, 64), 64), :] = tok[...]
     labs[me.tn] = lab[...]
-    sent += gather_tensor(me, [(tok, tblock, ts, tr), (lab, lblock, ls, lr)])
-    order = (2, 1, 3, 0)
     tx = []
-    for k, d in enumerate(order):
-        rows = pl.ds(pl.multiple_of(256 * up4(me.y, d), 256), 256)
-        tx.append(push(T.at[rows], Tp.at[rows], cs.at[k], cr.at[k], mate))
+
+    def share_plane(d):
+        rows = pl.ds(pl.multiple_of(256 * up4(me.zl, 4 - d), 256), 256)
+        tx.append(push(T.at[rows], Tp.at[rows], cs.at[d], cr.at[d], mate))
+
+    sent += gather_tensor(me, [(tok, tblock, ts, tr), (lab, lblock, ls, lr)], share_plane)
     for c in local:
         c.wait()
     for c in wx:
         c.wait_recv()
-    for c in tx:
-        c.wait_recv()
     sent += wx + tx
+
+    def mate_tokens(d):
+        y = up4(me.y, d)
+        k = up4(me.zl, 4 - y)
+        rows = pl.ds(pl.multiple_of(256 * y, 256), 256)
+        pltpu.make_async_remote_copy(
+            src_ref=T.at[rows], dst_ref=Tp.at[rows], send_sem=cs.at[k], recv_sem=cr.at[k],
+            device_id=mate, device_id_type=MESH,
+        ).wait_recv()
 
     starts = [sum(CHUNKS[:q]) for q in range(len(CHUNKS))]
 
@@ -160,6 +171,8 @@
 
     def first(q):
         a, n = starts[q], CHUNKS[q]
+        if q == 0:
+            mate_tokens(2)
         for i in range(2):
             o = 2 * a + i * n
             p = mult(i, q, 2)
@@ -167,18 +180,24 @@
             S[1, o:o + n, :] = p[:, 128:].astype(bf16)
         send(0, q, to_r)
         send(1, q, to_l)
+        if q == 0:
+            mate_tokens(1)
         for i in range(2):
             o = 2 * a + i * n
             p = mult(i, q, 1)
             K2[0, o:o + n, :] = p[:, :128]
             S[3, o:o + n, :] = p[:, 128:].astype(bf16)
         send(3, q, to_r)
+        if q == 0:
+            mate_tokens(3)
         for i in range(2):
             o = 2 * a + i * n
             p = mult(i, q, 3)
             K2[1, o:o + n, :] = p[:, 128:]
             S[4, o:o + n, :] = p[:, :128].astype(bf16)
         send(4, q, to_l)
+        if q == 0:
+            mate_tokens(0)
         for i in range(2):
             o = 2 * a + i * n
             PO[o:o + n, :] = mult(i, q, 0)
@@ -419,16 +438,16 @@
     return (sc[7] * inv) * (Y + last)
 
 
-def stats_kernel(outt, labs, erased, gram, coords, wall, ms, FY,
-                 zb, zg, X, XR, XS, XA, XF, GB,
+def stats_kernel(outt, labs, erased, gram, coords, wall, ms, rowbuf, FY,
+                 zb, zg, XG, RG, SG, ZG, AG, GB, XC, RC, SC, ZC, AC,
                  ws, wr, ms_s, ms_r, as_, ar, xs, xr, gs, gr):
     me = Spot()
     other = 1 - me.core
     mate = me.dpid(core=other)
-    chips = [(dy, dz) for dy in range(4) for dz in range(2) if dy or dz]
-    chip_dev = [me.dpid(y=up4(me.y, dy), zh=lax.rem(me.zh + dz, 2)) for dy, dz in chips]
+    across = me.dpid(zh=1 - me.zh)
+    y_dev = [me.dpid(y=up4(me.y, d)) for d in (1, 2, 3)]
     t_dev = [{"tensor": lax.rem(me.tn + d, 16)} for d in range(1, 16)]
-    greet(t_dev + chip_dev + [mate])
+    greet(t_dev + y_dev + [across, mate])
 
     out = outt[...]
     mean = jnp.sum(out, axis=1, keepdims=True) / TOKENS
@@ -437,7 +456,6 @@
     z = cen / spread
     for j in range(8):
         zb[j] = z[:, 128 * j:128 * j + 128].astype(bf16)
-    slot = 4 * me.x + me.zl
 
     def rows32(zl, x):
         return pl.ds(pl.multiple_of(32 * (4 * x + zl), 32), 32)
@@ -461,13 +479,15 @@
         acc = acc + nt(c1[:, cols], hot) + nt(c2[:, cols], hot) + nt(c3[:, cols], hot)
     wall[rows32(me.zl, me.x), :] = (acc / TOKENS / spread).astype(bf16)
     lane = lax.broadcasted_iota(jnp.int32, (32, 128), 1)
-    ms[rows32(me.zl, me.x), :] = jnp.where(lane < 64, mean, spread)
+    slot = 4 * me.x + me.zl
+    ms[slot, :, 0:32] = jnp.where(lane < 1, mean, spread).T[0:8]
+    ms[slot, :, 32:] = jnp.zeros((8, 96), f32)
 
     def wv(zl, x):
         return wall.at[rows32(zl, x)]
 
     def mv(zl, x):
-        return ms.at[rows32(zl, x)]
+        return ms.at[4 * x + zl]
 
     sent = gather_tensor(
         me, [(wv(me.zl, me.x), wv, ws, wr), (mv(me.zl, me.x), mv, ms_s, ms_r)]
@@ -483,43 +503,54 @@
     C = jnp.dot(wt, zall, preferred_element_type=f32)
     gram[...] = G
     lane = lax.broadcasted_iota(jnp.int32, (128, 128), 1)
-    X[0:128, :] = jnp.where(lane < 64, C[:128], pltpu.roll(C[128:], 64, 1))
+    XC[...] = jnp.where(lane < 64, C[:128], pltpu.roll(C[128:], 64, 1))
     mine = pl.ds(pl.multiple_of(16 * me.tn, 16), 16)
-    X[128:144, :] = gram[mine, 0:128]
-    X[144:160, :] = gram[mine, 128:256]
-    half = lambda c: pl.ds(pl.multiple_of(80 * c, 8), 80)
-    c0 = push(X.at[half(other)], XR, xs.at[0], xr.at[0], mate)
-    c0.wait_recv()
-    chip = me.y * 2 + me.zh
-    XS[...] = X[half(me.core), :] + XR[...]
-    XA[chip] = XS[...]
-    xc = []
-    for k, dev in enumerate(chip_dev):
-        xc.append(push(XS, XA.at[chip], xs.at[1 + k], xr.at[1 + k], dev))
-    for c in xc:
-        c.wait_recv()
-    tot = XA[0]
-    for k in range(1, 8):
-        tot = tot + XA[k]
-    XF[half(me.core), :] = tot
-    c1x = push(XF.at[half(me.core)], XF.at[half(me.core)], xs.at[8], xr.at[8], mate)
-    c1x.wait_recv()
-    GB[me.tn] = XF[128:160, :]
+    XG[0:16, :] = gram[mine, 0:128]
+    XG[16:32, :] = gram[mine, 128:256]
+    chains = ((16, XG, RG, SG, ZG, AG, GB.at[me.tn]), (64, XC, RC, SC, ZC, AC, coords))
+
+    def half(n, c):
+        return pl.ds(pl.multiple_of(n * c, 8), n)
+
+    cp = {}
+    for i, (n, X, R, *_) in enumerate(chains):
+        cp[i, 0] = push(X.at[half(n, other)], R, xs.at[i, 0], xr.at[i, 0], mate)
+    for i, (n, X, R, SS, Z, *_) in enumerate(chains):
+        cp[i, 0].wait_recv()
+        SS[...] = X[half(n, me.core), :] + R[...]
+        cp[i, 1] = push(SS, Z, xs.at[i, 1], xr.at[i, 1], across)
+    for i, (n, _, _, SS, Z, A, _) in enumerate(chains):
+        cp[i, 1].wait_recv()
+        A[me.y] = SS[...] + Z[...]
+        for k, dev in enumerate(y_dev):
+            cp[i, 2 + k] = push(A.at[me.y], A.at[me.y], xs.at[i, 2 + k], xr.at[i, 2 + k], dev)
+
+    def finish(i):
+        n, A, out = chains[i][0], chains[i][5], chains[i][6]
+        for k in range(3):
+            cp[i, 2 + k].wait_recv()
+        own = half(n, me.core)
+        out[own, :] = A[0] + A[1] + A[2] + A[3]
+        cp[i, 5] = push(out.at[own], out.at[own], xs.at[i, 5], xr.at[i, 5], mate)
 
     def gv(zl, x):
         return GB.at[4 * zl + x]
 
+    finish(0)
+    cp[0, 5].wait_recv()
     sent += gather_tensor(me, [(gv(me.zl, me.x), gv, gs, gr)])
+    finish(1)
     for t in range(16):
         gram[16 * t:16 * t + 16, 0:128] = GB[t, 0:16, :]
         gram[16 * t:16 * t + 16, 128:256] = GB[t, 16:32, :]
-    coords[0:128, :] = XF[0:128, :]
-    coords[128:256, :] = pltpu.roll(XF[0:128, :], 64, 1)
+        rowbuf[:, 32 * t:32 * t + 32] = ms[t, :, 0:32]
+    cp[1, 5].wait_recv()
+    coords[128:256, :] = pltpu.roll(coords[0:128, :], 64, 1)
     solved = solve(FY, gram, coords)
     fix = jnp.dot(wall[...], solved.astype(bf16), preferred_element_type=f32)
-    done = ms[:, 0:1] + ms[:, 64:65] * (zz - fix)
-    erased[...] = done.T[:64].astype(bf16)
-    for c in [*sent, c0, *xc, c1x]:
+    rest = (zz - fix).T[:64]
+    erased[...] = (rowbuf[0:1, :] + rowbuf[1:2, :] * rest).astype(bf16)
+    for c in [*sent, *cp.values()]:
         c.wait_send()
 
 
@@ -574,11 +605,13 @@
         in_specs=[VM, VM],
         out_specs=VM,
         scratch_shapes=[
-            V((256, 256), f32), V((256, 128), f32), V((512, 256), bf16), V((512, 128), f32), V((256, 384), f32),
-            V((8, 32, 128), bf16), V((512, 128), bf16), V((160, 128), f32), V((80, 128), f32),
-            V((80, 128), f32), V((8, 80, 128), f32), V((160, 128), f32), V((16, 32, 128), f32),
+            V((256, 256), f32), V((256, 128), f32), V((512, 256), bf16), V((16, 8, 128), f32), V((8, 512), f32),
+            V((256, 384), f32), V((8, 32, 128), bf16), V((512, 128), bf16),
+            V((32, 128), f32), V((16, 128), f32), V((16, 128), f32), V((16, 128), f32), V((4, 16, 128), f32),
+            V((16, 32, 128), f32),
+            V((128, 128), f32), V((64, 128), f32), V((64, 128), f32), V((64, 128), f32), V((4, 64, 128), f32),
             DMA((16,)), DMA((16,)), DMA((16,)), DMA((16,)), DMA((15,)), DMA((15,)),
-            DMA((9,)), DMA((9,)), DMA((16,)), DMA((16,)),
+            DMA((2, 6)), DMA((2, 6)), DMA((16,)), DMA((16,)),
         ],
         compiler_params=params(2),
         name="stats_solve_erase",

time: 169 us -> 170 us (level)
  Pallas kernels: 165 us -> 167 us
where the time goes in v3:
time: 170 us; the launch traced here: 169 us
  Pallas kernels  167 us (98%)
  local copies, waits for them, and re-layouts  2.07 us (1%)
    pallas_call x1, Pallas kernels, shards(): pl.pallas_call(hidden_kernel, out_shape=(S((UNITS, 128), bf16), S((16, 8,...  71.1 us
    pallas_call x1, Pallas kernels, shards(): pl.pallas_call(stats_kernel, out_shape=S((64, 512), bf16), in_specs=[VM,...  49.5 us
    pallas_call x1, Pallas kernels, shards(): pl.pallas_call(down_kernel, out_shape=S((32, 1024), f32), in_specs=[VM, A...  46 us

profile of v3, /device:TPU:1, one launch (start us, length us, event | category | flops | bytes accessed | tf_op | source)
XLA Modules:
  0.0 169.5 jit_solution(2610955546759900657)
XLA Ops:
  0.0 0.8 compare_select_fusion
  0.8 0.6 broadcast_in_dim.4.lab
  1.4 71.1 %gate_up_hidden.1 = (bf16[928,128]{1,0:T(8,128)(2,1)}, s32[16,8,128]{2,1,0:T(8,128)}) custom-call(bf16[64,512]{1,0:T(8,128)(2,1)} %tok.1, s32[8,128]{1,0:T(8,128)} %broadcast_in_dim.4.lab, bf16[1848,512]{1,0:T(8,128)(2,1)} %bitcast.2, bf16[1848,512]{1,0:T(8,128)(2,1)} %bitcast.3), custom_call_target="tpu_custom_call" | custom-call | tf_op jit(solution)/shard_map/gate_up_hidden/pallas_call | solution.py:572
  72.5 46.0 %down_scatter.1.outt = f32[32,1024]{1,0:T(8,128)} custom-call(bf16[928,128]{1,0:T(8,128)(2,1)} %get-tuple-element.7.h, bf16[1848,512]{1,0:T(8,128)(2,1)} %down.1), custom_call_target="tpu_custom_call" | custom-call | tf_op jit(solution)/shard_map/down_scatter/pallas_call | solution.py:587
  118.5 49.5 %stats_solve_erase.1 = bf16[64,512]{1,0:T(8,128)(2,1)} custom-call(f32[32,1024]{1,0:T(8,128)} %down_scatter.1.outt, s32[16,8,128]{2,1,0:T(8,128)} %get-tuple-element.8.labs), custom_call_target="tpu_custom_call" | custom-call | tf_op jit(solution)/shard_map/stats_solve_erase/pallas_call | solution.py:602
  168.0 1.5 copy.7

commit v4 on v3

--- a/solution.py
+++ b/solution.py
@@ -12,7 +12,8 @@
 TOKENS = 1024
 UNITS = 928
 SHIFT = 920
-CHUNKS = (240, 240, 224, 224)
+CHUNKS = (176, 176, 176, 160, 128, 112)
+HALF = 464
 epsilon = 1e-05
 ridge_share = 0.5
 f32 = jnp.float32
@@ -265,21 +266,34 @@
     xr, xl = me.tid(x=up4(me.x, 1)), me.tid(x=up4(me.x, 3))
     greet(tensor_peers(me) + [to_r, to_l, across, mate])
 
-    def hv(i, y, zh):
-        return H.at[i, y, pl.ds(0, UNITS), pl.ds(pl.multiple_of(128 * zh, 128), 128)]
+    def hv(i, y, zh, p):
+        return H.at[i, y, pl.ds(HALF * p, HALF), pl.ds(pl.multiple_of(128 * zh, 128), 128)]
+
+    def own(p):
+        return h.at[pl.ds(HALF * p, HALF)]
 
     zh, zo = me.zh, 1 - me.zh
     sent = []
-    cc = {}
-
-    def share(k, src, y, z):
-        cc[k] = push(src, hv(1, y, z), cs.at[k], cr.at[k], mate)
-        sent.append(cc[k])
-
-    cz = push(h, hv(0, me.y, zh), hs.at[0], hr.at[0], across)
-    cr0 = push(h, hv(0, me.y, zh), hs.at[1], hr.at[1], to_r)
-    cl0 = push(h, hv(0, me.y, zh), hs.at[2], hr.at[2], to_l)
-    share(0, h, me.y, zh)
+    hc, cc = {}, {}
+
+    def move(k, p, src, y, z, dev):
+        hc[k, p] = push(src, hv(0, y, z, p), hs.at[k, p], hr.at[k, p], dev)
+
+    def share(k, p, src, y, z):
+        cc[k, p] = push(src, hv(1, y, z, p), cs.at[k, p], cr.at[k, p], mate)
+        sent.append(cc[k, p])
+
+    def landed(*ks):
+        for k in ks:
+            for p in range(2):
+                cc[k, p].wait_recv()
+
+    for p in range(2):
+        move(0, p, own(p), me.y, zh, across)
+        move(1, p, own(p), me.y, zh, to_r)
+        move(2, p, own(p), me.y, zh, to_l)
+    for p in range(2):
+        share(0, p, own(p), me.y, zh)
     H[0, me.y, 0:UNITS, pl.ds(pl.multiple_of(128 * zh, 128), 128)] = h[...]
     H[:, :, UNITS:, :] = jnp.zeros((2, 4, 1024 - UNITS, 256), bf16)
     for i in range(2):
@@ -291,17 +305,19 @@
         D[i, 0:16, :] = jnp.where(jnp.logical_and(dup, row < 8), 0.0, head).astype(bf16)
         for k in range(4):
             DT[i, :, 256 * k:256 * k + 256] = D[i, 256 * k:256 * k + 256, :].T
-    cz.wait_recv()
-    v = hv(0, me.y, zo)
-    cr1 = push(v, v, hs.at[3], hr.at[3], to_r)
-    cl1 = push(v, v, hs.at[4], hr.at[4], to_l)
-    share(1, v, me.y, zo)
-    cr0.wait_recv()
-    v = hv(0, yl, zh)
-    fr = push(v, v, hs.at[5], hr.at[5], to_r)
-    share(2, v, yl, zh)
-    cl0.wait_recv()
-    share(3, hv(0, yr, zh), yr, zh)
+    for p in range(2):
+        hc[1, p].wait_recv()
+        v = hv(0, yl, zh, p)
+        move(5, p, v, yl, zh, to_r)
+        share(2, p, v, yl, zh)
+        hc[2, p].wait_recv()
+        share(3, p, hv(0, yr, zh, p), yr, zh)
+    for p in range(2):
+        hc[0, p].wait_recv()
+        v = hv(0, me.y, zo, p)
+        move(3, p, v, me.y, zo, to_r)
+        move(4, p, v, me.y, zo, to_l)
+        share(1, p, v, me.y, zo)
 
     oc = {}
 
@@ -362,30 +378,29 @@
                 tot = tot + RZ[g, d, b].astype(f32)
             outt[:, pl.ds(pl.multiple_of(256 * y + 128 * b, 128), 128)] = tot
 
-    cc[0].wait_recv()
-    cc[1].wait_recv()
+    landed(0, 1)
     group(0, me.y)
-    cl1.wait_recv()
-    v = hv(0, yr, zo)
-    fl = push(v, v, hs.at[6], hr.at[6], to_l)
-    share(4, v, yr, zo)
-    cr1.wait_recv()
-    share(5, hv(0, yl, zo), yl, zo)
-    cc[3].wait_recv()
-    cc[4].wait_recv()
+    for p in range(2):
+        hc[4, p].wait_recv()
+        v = hv(0, yr, zo, p)
+        move(6, p, v, yr, zo, to_l)
+        share(4, p, v, yr, zo)
+        hc[3, p].wait_recv()
+        share(5, p, hv(0, yl, zo, p), yl, zo)
+    landed(3, 4)
     group(1, yr)
     relay(0)
-    cc[2].wait_recv()
-    cc[5].wait_recv()
+    landed(2, 5)
     group(2, yl)
     relay(1)
-    fr.wait_recv()
-    share(6, hv(0, yf, zh), yf, zh)
+    for p in range(2):
+        hc[5, p].wait_recv()
+        share(6, p, hv(0, yf, zh, p), yf, zh)
     settle(0)
-    fl.wait_recv()
-    share(7, hv(0, yf, zo), yf, zo)
-    cc[6].wait_recv()
-    cc[7].wait_recv()
+    for p in range(2):
+        hc[6, p].wait_recv()
+        share(7, p, hv(0, yf, zo, p), yf, zo)
+    landed(6, 7)
     group(3, yf)
     relay(2)
     settle(1)
@@ -396,7 +411,7 @@
     close(1, yr)
     close(2, yl)
     close(3, yf)
-    for c in [*sent, cz, cr0, cl0, cr1, cl1, fr, fl, *oc.values(), *zc.values()]:
+    for c in [*sent, *hc.values(), *oc.values(), *zc.values()]:
         c.wait_send()
 
 
@@ -593,7 +608,7 @@
             V((2, 1024, 512), bf16), V((2, 512, 1024), bf16), V((2, 4, 1024, 256), bf16),
             V((512, 256), f32), V((4, 4, 128, 128), f32), V((4, 6, 128, 128), bf16),
             V((4, 6, 128, 128), bf16), V((4, 2, 128, 128), bf16), V((4, 3, 2, 32, 128), bf16),
-            DMA((2,)), DMA((7,)), DMA((7,)), DMA((8,)), DMA((8,)),
+            DMA((2,)), DMA((7, 2)), DMA((7, 2)), DMA((8, 2)), DMA((8, 2)),
             DMA((4, 6)), DMA((4, 6)), DMA((4, 3)), DMA((4, 3)),
         ],
         compiler_params=params(1),

time: 170 us -> 163 us (0.959)
  Pallas kernels: 167 us -> 160 us
    pallas_call x1, Pallas kernels: 46 us -> 42 us  [shards(): pl.pallas_call(down_kernel, out_shape=S((32, 1024), f32), in_specs=[VM, A...]
    pallas_call x1, Pallas kernels: 49.5 us -> 47.1 us  [shards(): pl.pallas_call(stats_kernel, out_shape=S((64, 512), bf16), in_specs=[VM,...]
where the time goes in v4:
time: 163 us
  Pallas kernels  160 us (98%)
  local copies, waits for them, and re-layouts  2.07 us (1%)
    pallas_call x1, Pallas kernels, shards(): pl.pallas_call(hidden_kernel, out_shape=(S((UNITS, 128), bf16), S((16, 8,...  70.7 us
    pallas_call x1, Pallas kernels, shards(): pl.pallas_call(stats_kernel, out_shape=S((64, 512), bf16), in_specs=[VM,...  47.1 us
    pallas_call x1, Pallas kernels, shards(): pl.pallas_call(down_kernel, out_shape=S((32, 1024), f32), in_specs=[VM, A...  42 us

profile of v4, /device:TPU:1, one launch (start us, length us, event | category | flops | bytes accessed | tf_op | source)
XLA Modules:
  0.0 162.7 jit_solution(3261686731120125341)
XLA Ops:
  0.0 0.8 compare_select_fusion
  0.8 0.6 broadcast_in_dim.4.lab
  1.4 70.7 %gate_up_hidden.1 = (bf16[928,128]{1,0:T(8,128)(2,1)}, s32[16,8,128]{2,1,0:T(8,128)}) custom-call(bf16[64,512]{1,0:T(8,128)(2,1)} %tok.1, s32[8,128]{1,0:T(8,128)} %broadcast_in_dim.4.lab, bf16[1848,512]{1,0:T(8,128)(2,1)} %bitcast.2, bf16[1848,512]{1,0:T(8,128)(2,1)} %bitcast.3), custom_call_target="tpu_custom_call" | custom-call | tf_op jit(solution)/shard_map/gate_up_hidden/pallas_call | solution.py:587
  72.1 42.0 %down_scatter.1.outt = f32[32,1024]{1,0:T(8,128)} custom-call(bf16[928,128]{1,0:T(8,128)(2,1)} %get-tuple-element.7.h, bf16[1848,512]{1,0:T(8,128)(2,1)} %down.1), custom_call_target="tpu_custom_call" | custom-call | tf_op jit(solution)/shard_map/down_scatter/pallas_call | solution.py:602
  114.1 47.1 %stats_solve_erase.1 = bf16[64,512]{1,0:T(8,128)(2,1)} custom-call(f32[32,1024]{1,0:T(8,128)} %down_scatter.1.outt, s32[16,8,128]{2,1,0:T(8,128)} %get-tuple-element.8.labs), custom_call_target="tpu_custom_call" | custom-call | tf_op jit(solution)/shard_map/stats_solve_erase/pallas_call | solution.py:617
  161.2 1.5 copy.7

commit v5 on v4

--- a/solution.py
+++ b/solution.py
@@ -12,8 +12,8 @@
 TOKENS = 1024
 UNITS = 928
 SHIFT = 920
-CHUNKS = (176, 176, 176, 160, 128, 112)
-HALF = 464
+CHUNKS = (160, 144, 128, 128, 112, 96, 80, 80)
+EDGES = (0, 240, 480, 704, 928)
 epsilon = 1e-05
 ridge_share = 0.5
 f32 = jnp.float32
@@ -242,7 +242,9 @@
             second(i - 1)
         if i >= 2:
             third(i - 2)
-    for q in range(nq):
+        if i >= 4:
+            last(i - 4)
+    for q in range(nq - 2, nq):
         last(q)
     for c in [*sent, *cps.values(), *zc.values()]:
         c.wait_send()
@@ -267,10 +269,10 @@
     greet(tensor_peers(me) + [to_r, to_l, across, mate])
 
     def hv(i, y, zh, p):
-        return H.at[i, y, pl.ds(HALF * p, HALF), pl.ds(pl.multiple_of(128 * zh, 128), 128)]
+        return H.at[i, y, pl.ds(EDGES[p], EDGES[p + 1] - EDGES[p]), pl.ds(pl.multiple_of(128 * zh, 128), 128)]
 
     def own(p):
-        return h.at[pl.ds(HALF * p, HALF)]
+        return h.at[pl.ds(EDGES[p], EDGES[p + 1] - EDGES[p])]
 
     zh, zo = me.zh, 1 - me.zh
     sent = []
@@ -285,14 +287,14 @@
 
     def landed(*ks):
         for k in ks:
-            for p in range(2):
+            for p in range(4):
                 cc[k, p].wait_recv()
 
-    for p in range(2):
+    for p in range(4):
         move(0, p, own(p), me.y, zh, across)
         move(1, p, own(p), me.y, zh, to_r)
         move(2, p, own(p), me.y, zh, to_l)
-    for p in range(2):
+    for p in range(4):
         share(0, p, own(p), me.y, zh)
     H[0, me.y, 0:UNITS, pl.ds(pl.multiple_of(128 * zh, 128), 128)] = h[...]
     H[:, :, UNITS:, :] = jnp.zeros((2, 4, 1024 - UNITS, 256), bf16)
@@ -305,14 +307,14 @@
         D[i, 0:16, :] = jnp.where(jnp.logical_and(dup, row < 8), 0.0, head).astype(bf16)
         for k in range(4):
             DT[i, :, 256 * k:256 * k + 256] = D[i, 256 * k:256 * k + 256, :].T
-    for p in range(2):
+    for p in range(4):
         hc[1, p].wait_recv()
         v = hv(0, yl, zh, p)
         move(5, p, v, yl, zh, to_r)
         share(2, p, v, yl, zh)
         hc[2, p].wait_recv()
         share(3, p, hv(0, yr, zh, p), yr, zh)
-    for p in range(2):
+    for p in range(4):
         hc[0, p].wait_recv()
         v = hv(0, me.y, zo, p)
         move(3, p, v, me.y, zo, to_r)
@@ -380,7 +382,7 @@
 
     landed(0, 1)
     group(0, me.y)
-    for p in range(2):
+    for p in range(4):
         hc[4, p].wait_recv()
         v = hv(0, yr, zo, p)
         move(6, p, v, yr, zo, to_l)
@@ -393,11 +395,11 @@
     landed(2, 5)
     group(2, yl)
     relay(1)
-    for p in range(2):
+    for p in range(4):
         hc[5, p].wait_recv()
         share(6, p, hv(0, yf, zh, p), yf, zh)
     settle(0)
-    for p in range(2):
+    for p in range(4):
         hc[6, p].wait_recv()
         share(7, p, hv(0, yf, zo, p), yf, zo)
     landed(6, 7)
@@ -608,7 +610,7 @@
             V((2, 1024, 512), bf16), V((2, 512, 1024), bf16), V((2, 4, 1024, 256), bf16),
             V((512, 256), f32), V((4, 4, 128, 128), f32), V((4, 6, 128, 128), bf16),
             V((4, 6, 128, 128), bf16), V((4, 2, 128, 128), bf16), V((4, 3, 2, 32, 128), bf16),
-            DMA((2,)), DMA((7, 2)), DMA((7, 2)), DMA((8, 2)), DMA((8, 2)),
+            DMA((2,)), DMA((7, 4)), DMA((7, 4)), DMA((8, 4)), DMA((8, 4)),
             DMA((4, 6)), DMA((4, 6)), DMA((4, 3)), DMA((4, 3)),
         ],
         compiler_params=params(1),

time: 163 us -> 161 us (0.988)
  Pallas kernels: 160 us -> 158 us
    pallas_call x1, Pallas kernels: 70.7 us -> 68 us  [shards(): pl.pallas_call(hidden_kernel, out_shape=(S((UNITS, 128), bf16), S((16, 8,...]
where the time goes in v5:
time: 161 us
  Pallas kernels  158 us (98%)
  local copies, waits for them, and re-layouts  2.07 us (1%)
    pallas_call x1, Pallas kernels, shards(): pl.pallas_call(hidden_kernel, out_shape=(S((UNITS, 128), bf16), S((16, 8,...  68 us
    pallas_call x1, Pallas kernels, shards(): pl.pallas_call(stats_kernel, out_shape=S((64, 512), bf16), in_specs=[VM,...  46.6 us
    pallas_call x1, Pallas kernels, shards(): pl.pallas_call(down_kernel, out_shape=S((32, 1024), f32), in_specs=[VM, A...  43.5 us

profile of v5, /device:TPU:1, one launch (start us, length us, event | category | flops | bytes accessed | tf_op | source)
XLA Modules:
  0.0 161.0 jit_solution(13188233184590929077)
XLA Ops:
  0.0 0.8 compare_select_fusion
  0.8 0.6 broadcast_in_dim.4.lab
  1.4 68.0 %gate_up_hidden.1 = (bf16[928,128]{1,0:T(8,128)(2,1)}, s32[16,8,128]{2,1,0:T(8,128)}) custom-call(bf16[64,512]{1,0:T(8,128)(2,1)} %tok.1, s32[8,128]{1,0:T(8,128)} %broadcast_in_dim.4.lab, bf16[1848,512]{1,0:T(8,128)(2,1)} %bitcast.2, bf16[1848,512]{1,0:T(8,128)(2,1)} %bitcast.3), custom_call_target="tpu_custom_call" | custom-call | tf_op jit(solution)/shard_map/gate_up_hidden/pallas_call | solution.py:589
  69.4 43.5 %down_scatter.1.outt = f32[32,1024]{1,0:T(8,128)} custom-call(bf16[928,128]{1,0:T(8,128)(2,1)} %get-tuple-element.7.h, bf16[1848,512]{1,0:T(8,128)(2,1)} %down.1), custom_call_target="tpu_custom_call" | custom-call | tf_op jit(solution)/shard_map/down_scatter/pallas_call | solution.py:604
  112.9 46.6 %stats_solve_erase.1 = bf16[64,512]{1,0:T(8,128)(2,1)} custom-call(f32[32,1024]{1,0:T(8,128)} %down_scatter.1.outt, s32[16,8,128]{2,1,0:T(8,128)} %get-tuple-element.8.labs), custom_call_target="tpu_custom_call" | custom-call | tf_op jit(solution)/shard_map/stats_solve_erase/pallas_call | solution.py:619
  159.5 1.5 copy.7
